TPU v7x, 512 devices: a whole 4x8x8 slice. The times are simulated.
512 devices in a mesh: tok: 128 (over z, y, core), head: 4 (over x).
Axes of the slice: x: 4, y: 8, z: 8, core: 2. Of those that a mesh axis runs over, the one named last changes fastest.
Arguments:
- tokens: bfloat16 [16384, 1536], P('tok'), may hold values from -6 to 6
- norm_gain: bfloat16 [1536], replicated, may hold values from 0.099609375 to 1.8984375
- w_query: bfloat16 [1536, 1536], P('tok', 'head')
- w_keyval: bfloat16 [1536, 256], P('tok')
- w_out: bfloat16 [1536, 1536], P('head', 'tok'), may hold values from -0.5 to 0.5
- segment_ids: int32 [16384], P('tok'), may hold values from 0 to 30, as said below
- lengths: int32 [31], replicated, may hold values from 128 to 1024, as said below
- member_prompt: int32 [384], P('head'), may hold values from 0 to 30
Outputs:
- mixed: bfloat16 [16384, 1536], P('tok', 'head')
- cycle_cache: bfloat16 [384, 1024, 256], P('head', 'tok')
Inputs may be any that keep to these rules, and one draw needn't show every extreme that they name: The prompts lie end to end in the order of lengths and their lengths sum to 16384; one prompt has exactly 1024 tokens and one exactly 128. `segment_ids`: segment_ids_t is the prompt that holds token t under lengths, so it never falls.
All inputs are finite; a program needn't handle non-finite values.
Results may differ from a plain program's by a relative error of at most 0.013.
Values may be sent and summed in bfloat16 or wider, within the bound.
No kernel may reach another device: no remote copies, remote signals or barrier semaphores. Data moves between devices by JAX's collectives and lax.ppermute only.
A program may use at most 64 MiB of HBM per device.

v0:
```python
import math
import jax
import jax.numpy as jnp
from jax import lax
from jax.sharding import PartitionSpec as P

HD = 128
WINDOW = 1024


def shifted(block, axis, distance):
    devices = range(lax.axis_size(axis))
    route = [(i - distance, i) for i in devices if i - distance in devices]
    return lax.ppermute(block, axis, route)


def rotate(values, positions):
    half_width = values.shape[-1] // 2
    frequency = 10000.0 ** (-(jnp.arange(half_width, dtype=jnp.float32) * 2.0 / values.shape[-1]))
    angles = positions.astype(jnp.float32)[:, None] * frequency[None, :]
    cosine = jnp.cos(angles)[:, None, :]
    sine_values = jnp.sin(angles)[:, None, :]
    front_half = values[..., :half_width]
    back_half = values[..., half_width:]
    return jnp.concatenate(
        [
            front_half * cosine - back_half * sine_values,
            back_half * cosine + front_half * sine_values,
        ],
        axis=-1,
    )


def lookup_table(segments, table):
    matches = segments[:, None] == jnp.arange(table.shape[0], dtype=jnp.int32)[None, :]
    return jnp.sum(jnp.where(matches, table[None, :], 0), axis=1)


def per_device(tokens, norm_gain, w_query, w_keyval, w_out, segment_ids, lengths, member_prompt):
    shard_rows = tokens.shape[0]
    heads_here = w_query.shape[1] // HD
    devices = lax.axis_size("tok")
    tok_index = lax.axis_index("tok")
    head_index = lax.axis_index("head")
    prompts = lengths.shape[0]
    prompt_ends = jnp.cumsum(lengths)
    starts = prompt_ends - lengths
    global_index = tok_index * shard_rows + jnp.arange(shard_rows, dtype=jnp.int32)
    positions = global_index - lookup_table(segment_ids, starts)
    widened = tokens.astype(jnp.float32)
    normed = (
        widened
        * lax.rsqrt(jnp.mean(widened * widened, axis=1, keepdims=True) + 1e-06)
        * norm_gain.astype(jnp.float32)
    ).astype(jnp.bfloat16)

    def add_rows(piece):
        return jnp.dot(normed, piece, preferred_element_type=jnp.float32)

    queries = add_rows(lax.all_gather(w_query, "tok", axis=0, tiled=True))
    queries = rotate(queries.reshape(shard_rows, heads_here, HD), positions).astype(jnp.bfloat16)
    keyval = add_rows(lax.all_gather(w_keyval, "tok", axis=0, tiled=True))
    rotated = rotate(keyval[:, None, :HD], positions)[:, 0]
    pairs = jnp.concatenate([rotated, keyval[:, HD:]], axis=1).astype(jnp.bfloat16)
    rim_shards = -(-WINDOW // shard_rows)
    rim_pairs = []
    rim_segments = []
    for distance in range(rim_shards, 0, -1):
        got_pairs, got_segments = shifted((pairs, segment_ids), "tok", distance)
        rim_pairs.append(got_pairs)
        rim_segments.append(got_segments)
    all_pairs = jnp.concatenate(rim_pairs + [pairs], axis=0)
    key_segments = jnp.concatenate(rim_segments + [segment_ids], axis=0)
    key_index = (tok_index - rim_shards) * shard_rows + jnp.arange(
        (rim_shards + 1) * shard_rows, dtype=jnp.int32
    )
    score_scale = 1.0 / math.sqrt(HD)
    outputs = []
    for head_slot in range(heads_here):
        query_head = queries[:, head_slot, :]
        scores = (
            jnp.einsum(
                "qd,kd->qk", query_head, all_pairs[:, :HD], preferred_element_type=jnp.float32
            )
            * score_scale
        )
        allowed = (key_segments[None, :] == segment_ids[:, None]) & (
            key_index[None, :] <= global_index[:, None]
        )
        allowed = (
            allowed
            & (key_index[None, :] > global_index[:, None] - WINDOW)
            & (key_index[None, :] >= 0)
        )
        scores = jnp.where(allowed, scores, -jnp.inf)
        largest = jnp.max(scores, axis=1, keepdims=True)
        weights = jnp.exp(scores - largest)
        total = jnp.sum(weights, axis=1, keepdims=True)
        probs = weights.astype(jnp.bfloat16)
        summed = jnp.dot(probs, all_pairs[:, HD:], preferred_element_type=jnp.float32)
        outputs.append((summed / total).astype(jnp.bfloat16))
    attention = jnp.concatenate(outputs, axis=1)
    quarter_cols = tokens.shape[1] // lax.axis_size("head")
    residual = lax.dynamic_slice_in_dim(tokens, head_index * quarter_cols, quarter_cols, 1).astype(
        jnp.float32
    )
    partial_out = jnp.dot(
        attention,
        lax.all_gather(w_out, "tok", axis=1, tiled=True),
        preferred_element_type=jnp.float32,
    )
    head_total = lax.psum_scatter(
        partial_out.astype(jnp.bfloat16), "head", scatter_dimension=1, tiled=True
    ).astype(jnp.float32)
    mixed = (residual + head_total).astype(jnp.bfloat16)
    slots_here = WINDOW // devices
    first_segment = jnp.sum((prompt_ends <= tok_index * shard_rows).astype(jnp.int32))
    slot_index = jnp.arange(WINDOW, dtype=jnp.int32)
    prompt_index = jnp.arange(prompts, dtype=jnp.int32)
    outgoing = []
    for local_seg in range(2):
        prompt_here = first_segment + local_seg
        matches = prompt_index == prompt_here
        prompt_size = jnp.sum(jnp.where(matches, lengths, 0))
        prompt_start = jnp.sum(jnp.where(matches, starts, 0))
        lowest = prompt_size - WINDOW
        places = lowest + jnp.mod(slot_index - lowest, WINDOW)
        local_rows = prompt_start + places - tok_index * shard_rows
        usable = (
            (prompt_here < prompts) & (places >= 0) & (local_rows >= 0) & (local_rows < shard_rows)
        )
        fetched = jnp.take(pairs, jnp.clip(local_rows, 0, shard_rows - 1), axis=0)
        kept = jnp.where(usable[:, None], fetched, jnp.zeros_like(fetched))
        outgoing.append(kept.reshape(devices, slots_here * 2 * HD))
    incoming = lax.all_to_all(jnp.stack(outgoing), "tok", split_axis=1, concat_axis=1, tiled=True)
    source_rows = jnp.arange(devices, dtype=jnp.int32) * shard_rows
    source_first = jnp.sum((prompt_ends[None, :] <= source_rows[:, None]).astype(jnp.int32), axis=1)
    owners = jnp.stack([source_first, source_first + 1]).reshape(-1)
    chooser = (owners[None, :] == prompt_index[:, None]).astype(jnp.bfloat16)
    slot_table = jnp.dot(
        chooser,
        incoming.reshape(2 * devices, slots_here * 2 * HD),
        preferred_element_type=jnp.float32,
    ).astype(jnp.bfloat16)
    member_pick = (member_prompt[:, None] == prompt_index[None, :]).astype(jnp.bfloat16)
    cycle_cache = jnp.dot(member_pick, slot_table, preferred_element_type=jnp.float32).astype(
        jnp.bfloat16
    )
    cycle_cache = cycle_cache.reshape(member_prompt.shape[0], slots_here, 2 * HD)
    return (mixed, cycle_cache)


def solution(mesh):
    return jax.shard_map(
        per_device,
        mesh=mesh,
        in_specs=(
            P("tok", None),
            P(),
            P("tok", "head"),
            P("tok", None),
            P("head", "tok"),
            P("tok"),
            P(),
            P("head"),
        ),
        out_specs=(P("tok", "head"), P("head", "tok", None)),
        check_vma=False,
    )
```

profile of v0, /device:TPU:8, one launch (start us, length us, event | category | flops | bytes accessed | tf_op | source)
XLA Modules:
  0.0 275.0 jit_solution(13498664107108925658)
XLA Ops:
  10.7 57.2 %all-gather.1 = bf16[128,12,256]{2,1,0:T(8,128)(2,1)S(1)} all-gather(bf16[1,12,256]{2,1,0:T(8,128)(2,1)} %bitcast.50), channel_id=1, replica_groups=mesh['tok'=128,'head'=4] {'tok'}, dimensions={0}, use_global_device_ids=true | all-gather | bytes 792576 | tf_op jit(solution)/shard_map/all_gather | solution.py:62
  71.7 6.0 %collective-permute-start.8 = (bf16[128,256]{0,1:T(8,128)(2,1)S(1)}, bf16[128,256]{0,1:T(8,128)(2,1)S(1)}, u32[]{:S(2)}, u32[]{:S(2)}) collective-permute-start(bf16[128,256]{0,1:T(8,128)(2,1)S(1)} %pad_maximum_fusion.1), channel_id=1, source_target_pairs={{0,32},{4,36},{8,40},{12,44},{16,48},{20,52},{24,56},{28,60},{32,6... | collective-permute-start | bytes 196616 | tf_op jit(solution)/shard_map/ppermute | solution.py:14
  77.8 3.4 %collective-permute-start.9 = (bf16[128,256]{0,1:T(8,128)(2,1)S(1)}, bf16[128,256]{0,1:T(8,128)(2,1)S(1)}, u32[]{:S(2)}, u32[]{:S(2)}) collective-permute-start(bf16[128,256]{0,1:T(8,128)(2,1)S(1)} %pad_maximum_fusion.1), channel_id=1, source_target_pairs={{0,28},{4,32},{8,36},{12,40},{16,44},{20,48},{24,52},{28,56},{32,6... | collective-permute-start | bytes 196616 | tf_op jit(solution)/shard_map/ppermute | solution.py:14
  81.2 4.8 %collective-permute-start.10 = (bf16[128,256]{0,1:T(8,128)(2,1)S(1)}, bf16[128,256]{0,1:T(8,128)(2,1)S(1)}, u32[]{:S(2)}, u32[]{:S(2)}) collective-permute-start(bf16[128,256]{0,1:T(8,128)(2,1)S(1)} %pad_maximum_fusion.1), channel_id=1, source_target_pairs={{0,24},{4,28},{8,32},{12,36},{16,40},{20,44},{24,48},{28,52},{32,5... | collective-permute-start | bytes 196616 | tf_op jit(solution)/shard_map/ppermute | solution.py:14
  86.0 3.2 %collective-permute-start.11 = (bf16[128,256]{0,1:T(8,128)(2,1)S(1)}, bf16[128,256]{0,1:T(8,128)(2,1)S(1)}, u32[]{:S(2)}, u32[]{:S(2)}) collective-permute-start(bf16[128,256]{0,1:T(8,128)(2,1)S(1)} %pad_maximum_fusion.1), channel_id=1, source_target_pairs={{0,20},{4,24},{8,28},{12,32},{16,36},{20,40},{24,44},{28,48},{32,5... | collective-permute-start | bytes 196616 | tf_op jit(solution)/shard_map/ppermute | solution.py:14
  89.2 5.1 %collective-permute-start = (s32[128]{0:T(128)S(1)}, s32[128]{0:T(128)S(1)}, u32[]{:S(2)}, u32[]{:S(2)}) collective-permute-start(s32[128]{0:T(128)S(1)} %copy-done.4), channel_id=1, source_target_pairs={{0,32},{4,36},{8,40},{12,44},{16,48},{20,52},{24,56},{28,60},{32,6... | collective-permute-start | bytes 1544 | tf_op jit(solution)/shard_map/ppermute | solution.py:14
  97.6 3.9 %gather_fusion = bf16[1024,256]{1,0:T(8,128)(2,1)S(1)} fusion(bf16[128,256]{1,0:T(8,128)(2,1)S(1)} %copy.46, s32[1024]{0:T(1024)S(1)} %get-tuple-element.27), kind=kCustom, calls=%fused_computation.clone | custom fusion | bytes 1052672 | tf_op jit(solution)/shard_map/jit(_take)/gather | solution.py:132
  104.8 3.9 %gather_fusion.1 = bf16[1024,256]{1,0:T(8,128)(2,1)S(1)} fusion(bf16[128,256]{1,0:T(8,128)(2,1)S(1)} %copy.46, s32[1024]{0:T(1024)S(1)} %get-tuple-element.28), kind=kCustom, calls=%fused_computation.1.clone | custom fusion | bytes 1052672 | tf_op jit(solution)/shard_map/jit(_take)/gather | solution.py:132
  109.3 3.2 %pad_maximum_fusion = bf16[2,128,2048]{2,0,1:T(2,128)(2,1)} fusion(bf16[1,128,2048]{2,0,1:T(2,128)(2,1)S(1)} %stack_reshape.9, bf16[1,128,2048]{2,0,1:T(2,128)(2,1)S(1)} %stack_reshape.8), kind=kLoop, calls=%fused_computation.17 | loop fusion | flops 2097152 | bytes 2097152 | tf_op jit(solution)/shard_map/stack | solution.py:135
  112.6 9.8 %all-to-all-start = ((bf16[2,128,2048]{2,0,1:T(2,128)(2,1)}), bf16[2,128,2048]{2,0,1:T(2,128)(2,1)S(1)}, u32[]{:S(2)}, u32[]{:S(2)}) async-start(bf16[2,128,2048]{2,0,1:T(2,128)(2,1)} %pad_maximum_fusion), calls=%async_computation | async-start | bytes 2097152 | tf_op jit(solution)/shard_map/all_to_all | solution.py:135
  123.4 6.1 %collective-permute-start.1 = (s32[128]{0:T(128)S(1)}, s32[128]{0:T(128)S(1)}, u32[]{:S(2)}, u32[]{:S(2)}) collective-permute-start(s32[128]{0:T(128)S(1)} %copy-done.4), channel_id=1, source_target_pairs={{0,28},{4,32},{8,36},{12,40},{16,44},{20,48},{24,52},{28,56},{32,6... | collective-permute-start | bytes 1544 | tf_op jit(solution)/shard_map/ppermute | solution.py:14
  129.5 14.7 %collective-permute-done.1 = s32[128]{0:T(128)S(1)} collective-permute-done((s32[128]{0:T(128)S(1)}, s32[128]{0:T(128)S(1)}, u32[]{:S(2)}, u32[]{:S(2)}) %collective-permute-start.1) | collective-permute-done | bytes 544 | tf_op jit(solution)/shard_map/ppermute | solution.py:14
  144.3 6.8 %collective-permute-start.2 = (s32[128]{0:T(128)S(1)}, s32[128]{0:T(128)S(1)}, u32[]{:S(2)}, u32[]{:S(2)}) collective-permute-start(s32[128]{0:T(128)S(1)} %copy-done.4), channel_id=1, source_target_pairs={{0,24},{4,28},{8,32},{12,36},{16,40},{20,44},{24,48},{28,52},{32,5... | collective-permute-start | bytes 1544 | tf_op jit(solution)/shard_map/ppermute | solution.py:14
  152.4 3.9 %collective-permute-start.3 = (s32[128]{0:T(128)S(1)}, s32[128]{0:T(128)S(1)}, u32[]{:S(2)}, u32[]{:S(2)}) collective-permute-start(s32[128]{0:T(128)S(1)} %copy-done.4), channel_id=1, source_target_pairs={{0,20},{4,24},{8,28},{12,32},{16,36},{20,40},{24,44},{28,48},{32,5... | collective-permute-start | bytes 1544 | tf_op jit(solution)/shard_map/ppermute | solution.py:14
  157.6 6.5 %collective-permute-start.4 = (s32[128]{0:T(128)S(1)}, s32[128]{0:T(128)S(1)}, u32[]{:S(2)}, u32[]{:S(2)}) collective-permute-start(s32[128]{0:T(128)S(1)} %copy-done.4), channel_id=1, source_target_pairs={{0,16},{4,20},{8,24},{12,28},{16,32},{20,36},{24,40},{28,44},{32,4... | collective-permute-start | bytes 1544 | tf_op jit(solution)/shard_map/ppermute | solution.py:14
  165.4 3.5 %collective-permute-start.5 = (s32[128]{0:T(128)S(1)}, s32[128]{0:T(128)S(1)}, u32[]{:S(2)}, u32[]{:S(2)}) collective-permute-start(s32[128]{0:T(128)S(1)} %copy-done.4), channel_id=1, source_target_pairs={{0,12},{4,16},{8,20},{12,24},{16,28},{20,32},{24,36},{28,40},{32,4... | collective-permute-start | bytes 1544 | tf_op jit(solution)/shard_map/ppermute | solution.py:14
  170.2 6.8 %collective-permute-start.6 = (s32[128]{0:T(128)S(1)}, s32[128]{0:T(128)S(1)}, u32[]{:S(2)}, u32[]{:S(2)}) collective-permute-start(s32[128]{0:T(128)S(1)} %copy-done.4), channel_id=1, source_target_pairs={{0,8},{4,12},{8,16},{12,20},{16,24},{20,28},{24,32},{28,36},{32,40... | collective-permute-start | bytes 1544 | tf_op jit(solution)/shard_map/ppermute | solution.py:14
  178.2 2.4 collective-permute-start.7
  180.6 2.5 collective-permute-done.7
  183.1 7.5 %collective-permute-start.12 = (bf16[128,256]{0,1:T(8,128)(2,1)S(1)}, bf16[128,256]{0,1:T(8,128)(2,1)S(1)}, u32[]{:S(2)}, u32[]{:S(2)}) collective-permute-start(bf16[128,256]{0,1:T(8,128)(2,1)S(1)} %pad_maximum_fusion.1), channel_id=1, source_target_pairs={{0,16},{4,20},{8,24},{12,28},{16,32},{20,36},{24,40},{28,44},{32,4... | collective-permute-start | bytes 196616 | tf_op jit(solution)/shard_map/ppermute | solution.py:14
  190.6 3.2 %collective-permute-start.13 = (bf16[128,256]{0,1:T(8,128)(2,1)S(1)}, bf16[128,256]{0,1:T(8,128)(2,1)S(1)}, u32[]{:S(2)}, u32[]{:S(2)}) collective-permute-start(bf16[128,256]{0,1:T(8,128)(2,1)S(1)} %pad_maximum_fusion.1), channel_id=1, source_target_pairs={{0,12},{4,16},{8,20},{12,24},{16,28},{20,32},{24,36},{28,40},{32,4... | collective-permute-start | bytes 196616 | tf_op jit(solution)/shard_map/ppermute | solution.py:14
  194.4 5.4 %collective-permute-start.14 = (bf16[128,256]{0,1:T(8,128)(2,1)S(1)}, bf16[128,256]{0,1:T(8,128)(2,1)S(1)}, u32[]{:S(2)}, u32[]{:S(2)}) collective-permute-start(bf16[128,256]{0,1:T(8,128)(2,1)S(1)} %pad_maximum_fusion.1), channel_id=1, source_target_pairs={{0,8},{4,12},{8,16},{12,20},{16,24},{20,28},{24,32},{28,36},{32,40... | collective-permute-start | bytes 196616 | tf_op jit(solution)/shard_map/ppermute | solution.py:14
  200.5 2.8 %collective-permute-start.15 = (bf16[128,256]{0,1:T(8,128)(2,1)S(1)}, bf16[128,256]{0,1:T(8,128)(2,1)S(1)}, u32[]{:S(2)}, u32[]{:S(2)}) collective-permute-start(bf16[128,256]{0,1:T(8,128)(2,1)S(1)} %pad_maximum_fusion.1), channel_id=1, source_target_pairs={{0,4},{4,8},{8,12},{12,16},{16,20},{20,24},{24,28},{28,32},{32,36}... | collective-permute-start | bytes 196616 | tf_op jit(solution)/shard_map/ppermute | solution.py:14
  227.0 39.8 %reduce-scatter.4.cloned.1.call-done = bf16[384,128]{1,0:T(8,128)(2,1)} async-done(((bf16[1536,128]{1,0:T(8,128)(2,1)}), bf16[384,128]{1,0:T(8,128)(2,1)}) %reduce-scatter.4.cloned.1.call-update) | async-done | bytes 98320
  (106 shorter events, 45.8 us)
Async XLA Ops:
  7.2 200.6 %all-gather.6.cloned.1.call-start = ((), (), s32[]{:S(2)}) async-start(), calls=%async_computation.2 | async-start | bytes 1585152 | tf_op jit(solution)/shard_map/all_gather | solution.py:60
  67.8 1.0 copy-start
  67.8 2.1 copy-start.2
  67.9 3.5 %copy-start.4 = (s32[128]{0:T(128)S(1)}, s32[128]{0:T(128)}, u32[]{:S(2)}) copy-start(s32[128]{0:T(128)} %param.15) | copy-start | bytes 1540
  71.7 118.9 %collective-permute-start.8 = (bf16[128,256]{0,1:T(8,128)(2,1)S(1)}, bf16[128,256]{0,1:T(8,128)(2,1)S(1)}, u32[]{:S(2)}, u32[]{:S(2)}) collective-permute-start(bf16[128,256]{0,1:T(8,128)(2,1)S(1)} %pad_maximum_fusion.1), channel_id=1, source_target_pairs={{0,32},{4,36},{8,40},{12,44},{16,48},{20,52},{24,56},{28,60},{32,6... | collective-permute-start | bytes 196616 | tf_op jit(solution)/shard_map/ppermute | solution.py:14
  77.8 116.7 %collective-permute-start.9 = (bf16[128,256]{0,1:T(8,128)(2,1)S(1)}, bf16[128,256]{0,1:T(8,128)(2,1)S(1)}, u32[]{:S(2)}, u32[]{:S(2)}) collective-permute-start(bf16[128,256]{0,1:T(8,128)(2,1)S(1)} %pad_maximum_fusion.1), channel_id=1, source_target_pairs={{0,28},{4,32},{8,36},{12,40},{16,44},{20,48},{24,52},{28,56},{32,6... | collective-permute-start | bytes 196616 | tf_op jit(solution)/shard_map/ppermute | solution.py:14
  81.2 119.3 %collective-permute-start.10 = (bf16[128,256]{0,1:T(8,128)(2,1)S(1)}, bf16[128,256]{0,1:T(8,128)(2,1)S(1)}, u32[]{:S(2)}, u32[]{:S(2)}) collective-permute-start(bf16[128,256]{0,1:T(8,128)(2,1)S(1)} %pad_maximum_fusion.1), channel_id=1, source_target_pairs={{0,24},{4,28},{8,32},{12,36},{16,40},{20,44},{24,48},{28,52},{32,5... | collective-permute-start | bytes 196616 | tf_op jit(solution)/shard_map/ppermute | solution.py:14
  86.0 117.9 %collective-permute-start.11 = (bf16[128,256]{0,1:T(8,128)(2,1)S(1)}, bf16[128,256]{0,1:T(8,128)(2,1)S(1)}, u32[]{:S(2)}, u32[]{:S(2)}) collective-permute-start(bf16[128,256]{0,1:T(8,128)(2,1)S(1)} %pad_maximum_fusion.1), channel_id=1, source_target_pairs={{0,20},{4,24},{8,28},{12,32},{16,36},{20,40},{24,44},{28,48},{32,5... | collective-permute-start | bytes 196616 | tf_op jit(solution)/shard_map/ppermute | solution.py:14
  89.2 34.2 %collective-permute-start = (s32[128]{0:T(128)S(1)}, s32[128]{0:T(128)S(1)}, u32[]{:S(2)}, u32[]{:S(2)}) collective-permute-start(s32[128]{0:T(128)S(1)} %copy-done.4), channel_id=1, source_target_pairs={{0,32},{4,36},{8,40},{12,44},{16,48},{20,52},{24,56},{28,60},{32,6... | collective-permute-start | bytes 1544 | tf_op jit(solution)/shard_map/ppermute | solution.py:14
  112.6 112.6 %all-to-all-start = ((bf16[2,128,2048]{2,0,1:T(2,128)(2,1)}), bf16[2,128,2048]{2,0,1:T(2,128)(2,1)S(1)}, u32[]{:S(2)}, u32[]{:S(2)}) async-start(bf16[2,128,2048]{2,0,1:T(2,128)(2,1)} %pad_maximum_fusion), calls=%async_computation | async-start | bytes 2097152 | tf_op jit(solution)/shard_map/all_to_all | solution.py:135
  122.4 92.1 %all-gather.8.cloned.1.call-start = ((), (), s32[]{:S(2)}) async-start(), calls=%async_computation.3 | async-start | bytes 1585152 | tf_op jit(solution)/shard_map/all_gather | solution.py:109
  123.1 143.7 %reduce-scatter.4.cloned.1.call-start = ((), (), s32[]{:S(2)}) async-start(), calls=%async_computation.4 | async-start | bytes 491520
  123.4 20.9 %collective-permute-start.1 = (s32[128]{0:T(128)S(1)}, s32[128]{0:T(128)S(1)}, u32[]{:S(2)}, u32[]{:S(2)}) collective-permute-start(s32[128]{0:T(128)S(1)} %copy-done.4), channel_id=1, source_target_pairs={{0,28},{4,32},{8,36},{12,40},{16,44},{20,48},{24,52},{28,56},{32,6... | collective-permute-start | bytes 1544 | tf_op jit(solution)/shard_map/ppermute | solution.py:14
  144.3 8.1 %collective-permute-start.2 = (s32[128]{0:T(128)S(1)}, s32[128]{0:T(128)S(1)}, u32[]{:S(2)}, u32[]{:S(2)}) collective-permute-start(s32[128]{0:T(128)S(1)} %copy-done.4), channel_id=1, source_target_pairs={{0,24},{4,28},{8,32},{12,36},{16,40},{20,44},{24,48},{28,52},{32,5... | collective-permute-start | bytes 1544 | tf_op jit(solution)/shard_map/ppermute | solution.py:14
  152.4 5.2 %collective-permute-start.3 = (s32[128]{0:T(128)S(1)}, s32[128]{0:T(128)S(1)}, u32[]{:S(2)}, u32[]{:S(2)}) collective-permute-start(s32[128]{0:T(128)S(1)} %copy-done.4), channel_id=1, source_target_pairs={{0,20},{4,24},{8,28},{12,32},{16,36},{20,40},{24,44},{28,48},{32,5... | collective-permute-start | bytes 1544 | tf_op jit(solution)/shard_map/ppermute | solution.py:14
  157.6 7.8 %collective-permute-start.4 = (s32[128]{0:T(128)S(1)}, s32[128]{0:T(128)S(1)}, u32[]{:S(2)}, u32[]{:S(2)}) collective-permute-start(s32[128]{0:T(128)S(1)} %copy-done.4), channel_id=1, source_target_pairs={{0,16},{4,20},{8,24},{12,28},{16,32},{20,36},{24,40},{28,44},{32,4... | collective-permute-start | bytes 1544 | tf_op jit(solution)/shard_map/ppermute | solution.py:14
  165.4 4.8 %collective-permute-start.5 = (s32[128]{0:T(128)S(1)}, s32[128]{0:T(128)S(1)}, u32[]{:S(2)}, u32[]{:S(2)}) collective-permute-start(s32[128]{0:T(128)S(1)} %copy-done.4), channel_id=1, source_target_pairs={{0,12},{4,16},{8,20},{12,24},{16,28},{20,32},{24,36},{28,40},{32,4... | collective-permute-start | bytes 1544 | tf_op jit(solution)/shard_map/ppermute | solution.py:14
  170.2 8.1 %collective-permute-start.6 = (s32[128]{0:T(128)S(1)}, s32[128]{0:T(128)S(1)}, u32[]{:S(2)}, u32[]{:S(2)}) collective-permute-start(s32[128]{0:T(128)S(1)} %copy-done.4), channel_id=1, source_target_pairs={{0,8},{4,12},{8,16},{12,20},{16,24},{20,28},{24,32},{28,36},{32,40... | collective-permute-start | bytes 1544 | tf_op jit(solution)/shard_map/ppermute | solution.py:14
  178.2 4.9 %collective-permute-start.7 = (s32[128]{0:T(128)S(1)}, s32[128]{0:T(128)S(1)}, u32[]{:S(2)}, u32[]{:S(2)}) collective-permute-start(s32[128]{0:T(128)S(1)} %copy-done.4), channel_id=1, source_target_pairs={{0,4},{4,8},{8,12},{12,16},{16,20},{20,24},{24,28},{28,32},{32,36}... | collective-permute-start | bytes 1544 | tf_op jit(solution)/shard_map/ppermute | solution.py:14
  183.1 21.4 %collective-permute-start.12 = (bf16[128,256]{0,1:T(8,128)(2,1)S(1)}, bf16[128,256]{0,1:T(8,128)(2,1)S(1)}, u32[]{:S(2)}, u32[]{:S(2)}) collective-permute-start(bf16[128,256]{0,1:T(8,128)(2,1)S(1)} %pad_maximum_fusion.1), channel_id=1, source_target_pairs={{0,16},{4,20},{8,24},{12,28},{16,32},{20,36},{24,40},{28,44},{32,4... | collective-permute-start | bytes 196616 | tf_op jit(solution)/shard_map/ppermute | solution.py:14
  190.6 14.6 %collective-permute-start.13 = (bf16[128,256]{0,1:T(8,128)(2,1)S(1)}, bf16[128,256]{0,1:T(8,128)(2,1)S(1)}, u32[]{:S(2)}, u32[]{:S(2)}) collective-permute-start(bf16[128,256]{0,1:T(8,128)(2,1)S(1)} %pad_maximum_fusion.1), channel_id=1, source_target_pairs={{0,12},{4,16},{8,20},{12,24},{16,28},{20,32},{24,36},{28,40},{32,4... | collective-permute-start | bytes 196616 | tf_op jit(solution)/shard_map/ppermute | solution.py:14
  194.4 11.4 %collective-permute-start.14 = (bf16[128,256]{0,1:T(8,128)(2,1)S(1)}, bf16[128,256]{0,1:T(8,128)(2,1)S(1)}, u32[]{:S(2)}, u32[]{:S(2)}) collective-permute-start(bf16[128,256]{0,1:T(8,128)(2,1)S(1)} %pad_maximum_fusion.1), channel_id=1, source_target_pairs={{0,8},{4,12},{8,16},{12,20},{16,24},{20,28},{24,32},{28,36},{32,40... | collective-permute-start | bytes 196616 | tf_op jit(solution)/shard_map/ppermute | solution.py:14
  200.5 6.0 %collective-permute-start.15 = (bf16[128,256]{0,1:T(8,128)(2,1)S(1)}, bf16[128,256]{0,1:T(8,128)(2,1)S(1)}, u32[]{:S(2)}, u32[]{:S(2)}) collective-permute-start(bf16[128,256]{0,1:T(8,128)(2,1)S(1)} %pad_maximum_fusion.1), channel_id=1, source_target_pairs={{0,4},{4,8},{8,12},{12,16},{16,20},{20,24},{24,28},{28,32},{32,36}... | collective-permute-start | bytes 196616 | tf_op jit(solution)/shard_map/ppermute | solution.py:14
  219.4 1.5 copy-start.1
  (1 other events, 0.7 us)
Sparse Core Ops, SparseCore 0:
  11.2 89.9 all-gather.5
  126.4 84.7 all-gather.7
  225.2 41.6 reduce-scatter.3
where the time goes:
time: 276 us; the launch traced here: 275 us
  starting transfers between devices  87.2 us (32%)
  waiting for transfers between devices  64.8 us (23%)
  blocking collectives  57.2 us (21%)
  local copies, waits for them, and re-layouts  22.6 us (8%)
  between operations  16.8 us (6%)
  other arithmetic  15.6 us (6%)
  matrix products  10.9 us (4%)
    ppermute x16, starting transfers between devices, shifted(): return lax.ppermute(block, axis, route)  77.3 us
    all_gather x1, blocking collectives, per_device(): keyval = add_rows(lax.all_gather(w_keyval, 'tok', axis=0, tiled=True))  57.2 us
    unnamed x4, waiting for transfers between devices  41.2 us
    ppermute x16, waiting for transfers between devices, shifted(): return lax.ppermute(block, axis, route)  23.6 us
    unnamed x32, local copies, waits for them, and re-layouts  13 us
    all_to_all x1, starting transfers between devices, per_device(): lax.all_to_all(jnp.stack(outgoing), 'tok', split_axis=1, concat_axis=1, t...  9.78 us
    gather x2, local copies, waits for them, and re-layouts, per_device(): fetched = jnp.take(pairs, jnp.clip(local_rows, 0, shard_rows - 1), axis=0)  7.88 us
  transfers between devices with their start and end apart: 20, of which 8 were waited for; matrix products, arithmetic and copies ran while one was open for 17% of the time, Pallas kernels for 0%

commit v1 on v0

--- a/solution.py
+++ b/solution.py
@@ -59,7 +59,10 @@
 
     queries = add_rows(lax.all_gather(w_query, "tok", axis=0, tiled=True))
     queries = rotate(queries.reshape(shard_rows, heads_here, HD), positions).astype(jnp.bfloat16)
-    keyval = add_rows(lax.all_gather(w_keyval, "tok", axis=0, tiled=True))
+    derive_strips_all = lambda field_in: jnp.concatenate(
+        lax.all_to_all(jnp.stack([field_in for _ in range(lax.axis_size("tok"))]), "tok", 0, 0), 0
+    )
+    keyval = add_rows(derive_strips_all(w_keyval))
     rotated = rotate(keyval[:, None, :HD], positions)[:, 0]
     pairs = jnp.concatenate([rotated, keyval[:, HD:]], axis=1).astype(jnp.bfloat16)
     rim_shards = -(-WINDOW // shard_rows)

time: 276 us -> 249 us (0.902)
  the two profiles are of different devices: /device:TPU:8 before, /device:TPU:16 now
where the time goes in v1:
time: 249 us; the launch traced here: 248 us
  waiting for transfers between devices  102 us (41%)
  starting transfers between devices  88.9 us (36%)
  local copies, waits for them, and re-layouts  21 us (8%)
  between operations  17 us (7%)
  other arithmetic  12.3 us (5%)
  matrix products  6.58 us (3%)
    ppermute x16, starting transfers between devices, shifted(): return lax.ppermute(block, axis, route)  65 us
    all_gather x1, waiting for transfers between devices, per_device(): lax.all_gather(w_out, 'tok', axis=1, tiled=True)  49.3 us
    unnamed x4, waiting for transfers between devices  25 us
    ppermute x16, waiting for transfers between devices, shifted(): return lax.ppermute(block, axis, route)  19.7 us
    all_to_all x1, starting transfers between devices, per_device(): lax.all_to_all(jnp.stack([field_in for _ in range(lax.axis_size('tok'))])...  15.7 us
    unnamed x41, local copies, waits for them, and re-layouts  10.2 us
    all_to_all x1, starting transfers between devices, per_device(): lax.all_to_all(jnp.stack(outgoing), 'tok', split_axis=1, concat_axis=1, t...  8.12 us
    gather x2, local copies, waits for them, and re-layouts, per_device(): fetched = jnp.take(pairs, jnp.clip(local_rows, 0, shard_rows - 1), axis=0)  7.88 us
  transfers between devices with their start and end apart: 21, of which 8 were waited for; matrix products, arithmetic and copies ran while one was open for 15% of the time, Pallas kernels for 0%

profile of v1, /device:TPU:16, one launch (start us, length us, event | category | flops | bytes accessed | tf_op | source)
XLA Modules:
  0.0 247.8 jit_solution(16428527446908678231)
XLA Ops:
  7.9 5.9 %collective-permute-start = (s32[128]{0:T(128)}, s32[128]{0:T(128)S(1)}, u32[]{:S(2)}, u32[]{:S(2)}) collective-permute-start(s32[128]{0:T(128)} %param.15), channel_id=1, source_target_pairs={{0,32},{4,36},{8,40},{12,44},{16,48},{20,52},{24,56},{28,60},{32,6... | collective-permute-start | bytes 1544 | tf_op jit(solution)/shard_map/ppermute | solution.py:14
  13.8 3.8 %collective-permute-start.1 = (s32[128]{0:T(128)}, s32[128]{0:T(128)S(1)}, u32[]{:S(2)}, u32[]{:S(2)}) collective-permute-start(s32[128]{0:T(128)} %param.15), channel_id=1, source_target_pairs={{0,28},{4,32},{8,36},{12,40},{16,44},{20,48},{24,52},{28,56},{32,6... | collective-permute-start | bytes 1544 | tf_op jit(solution)/shard_map/ppermute | solution.py:14
  17.6 6.7 %collective-permute-start.2 = (s32[128]{0:T(128)}, s32[128]{0:T(128)S(1)}, u32[]{:S(2)}, u32[]{:S(2)}) collective-permute-start(s32[128]{0:T(128)} %param.15), channel_id=1, source_target_pairs={{0,24},{4,28},{8,32},{12,36},{16,40},{20,44},{24,48},{28,52},{32,5... | collective-permute-start | bytes 1544 | tf_op jit(solution)/shard_map/ppermute | solution.py:14
  24.3 3.1 %collective-permute-start.3 = (s32[128]{0:T(128)}, s32[128]{0:T(128)S(1)}, u32[]{:S(2)}, u32[]{:S(2)}) collective-permute-start(s32[128]{0:T(128)} %param.15), channel_id=1, source_target_pairs={{0,20},{4,24},{8,28},{12,32},{16,36},{20,40},{24,44},{28,48},{32,5... | collective-permute-start | bytes 1544 | tf_op jit(solution)/shard_map/ppermute | solution.py:14
  27.5 4.5 %collective-permute-start.4 = (s32[128]{0:T(128)}, s32[128]{0:T(128)S(1)}, u32[]{:S(2)}, u32[]{:S(2)}) collective-permute-start(s32[128]{0:T(128)} %param.15), channel_id=1, source_target_pairs={{0,16},{4,20},{8,24},{12,28},{16,32},{20,36},{24,40},{28,44},{32,4... | collective-permute-start | bytes 1544 | tf_op jit(solution)/shard_map/ppermute | solution.py:14
  33.7 15.7 %all-to-all-start = ((bf16[128,12,256]{2,1,0:T(8,128)(2,1)}), bf16[128,12,256]{2,1,0:T(8,128)(2,1)S(1)}, u32[]{:S(2)}, u32[]{:S(2)}) async-start(bf16[128,12,256]{2,1,0:T(8,128)(2,1)} %stack.8), calls=%async_computation | async-start | bytes 2097152 | tf_op jit(solution)/shard_map/all_to_all | solution.py:63
  59.6 3.1 %collective-permute-start.5 = (s32[128]{0:T(128)S(1)}, s32[128]{0:T(128)S(1)}, u32[]{:S(2)}, u32[]{:S(2)}) collective-permute-start(s32[128]{0:T(128)S(1)} %copy-done.9), channel_id=1, source_target_pairs={{0,12},{4,16},{8,20},{12,24},{16,28},{20,32},{24,36},{28,40},{32,4... | collective-permute-start | bytes 1544 | tf_op jit(solution)/shard_map/ppermute | solution.py:14
  62.7 4.6 %collective-permute-start.6 = (s32[128]{0:T(128)S(1)}, s32[128]{0:T(128)S(1)}, u32[]{:S(2)}, u32[]{:S(2)}) collective-permute-start(s32[128]{0:T(128)S(1)} %copy-done.9), channel_id=1, source_target_pairs={{0,8},{4,12},{8,16},{12,20},{16,24},{20,28},{24,32},{28,36},{32,40... | collective-permute-start | bytes 1544 | tf_op jit(solution)/shard_map/ppermute | solution.py:14
  72.4 7.9 %all-to-all-done = bf16[128,12,256]{2,1,0:T(8,128)(2,1)S(1)} async-done(((bf16[128,12,256]{2,1,0:T(8,128)(2,1)}), bf16[128,12,256]{2,1,0:T(8,128)(2,1)S(1)}, u32[]{:S(2)}, u32[]{:S(2)}) %all-to-all-start) | async-done | bytes 786464 | tf_op jit(solution)/shard_map/all_to_all | solution.py:63
  81.3 4.2 %collective-permute-start.8 = (bf16[128,256]{0,1:T(8,128)(2,1)S(1)}, bf16[128,256]{0,1:T(8,128)(2,1)}, u32[]{:S(2)}, u32[]{:S(2)}) collective-permute-start(bf16[128,256]{0,1:T(8,128)(2,1)S(1)} %pad_maximum_fusion.1), channel_id=1, source_target_pairs={{0,32},{4,36},{8,40},{12,44},{16,48},{20,52},{24,56},{28,60},{32,6... | collective-permute-start | bytes 196616 | tf_op jit(solution)/shard_map/ppermute | solution.py:14
  85.5 4.1 %collective-permute-start.9 = (bf16[128,256]{0,1:T(8,128)(2,1)S(1)}, bf16[128,256]{0,1:T(8,128)(2,1)S(1)}, u32[]{:S(2)}, u32[]{:S(2)}) collective-permute-start(bf16[128,256]{0,1:T(8,128)(2,1)S(1)} %pad_maximum_fusion.1), channel_id=1, source_target_pairs={{0,28},{4,32},{8,36},{12,40},{16,44},{20,48},{24,52},{28,56},{32,6... | collective-permute-start | bytes 196616 | tf_op jit(solution)/shard_map/ppermute | solution.py:14
  89.5 3.7 %collective-permute-start.10 = (bf16[128,256]{0,1:T(8,128)(2,1)S(1)}, bf16[128,256]{0,1:T(8,128)(2,1)S(1)}, u32[]{:S(2)}, u32[]{:S(2)}) collective-permute-start(bf16[128,256]{0,1:T(8,128)(2,1)S(1)} %pad_maximum_fusion.1), channel_id=1, source_target_pairs={{0,24},{4,28},{8,32},{12,36},{16,40},{20,44},{24,48},{28,52},{32,5... | collective-permute-start | bytes 196616 | tf_op jit(solution)/shard_map/ppermute | solution.py:14
  93.2 4.3 %collective-permute-start.11 = (bf16[128,256]{0,1:T(8,128)(2,1)S(1)}, bf16[128,256]{0,1:T(8,128)(2,1)S(1)}, u32[]{:S(2)}, u32[]{:S(2)}) collective-permute-start(bf16[128,256]{0,1:T(8,128)(2,1)S(1)} %pad_maximum_fusion.1), channel_id=1, source_target_pairs={{0,20},{4,24},{8,28},{12,32},{16,36},{20,40},{24,44},{28,48},{32,5... | collective-permute-start | bytes 196616 | tf_op jit(solution)/shard_map/ppermute | solution.py:14
  97.5 5.2 %collective-permute-start.12 = (bf16[128,256]{0,1:T(8,128)(2,1)S(1)}, bf16[128,256]{0,1:T(8,128)(2,1)S(1)}, u32[]{:S(2)}, u32[]{:S(2)}) collective-permute-start(bf16[128,256]{0,1:T(8,128)(2,1)S(1)} %pad_maximum_fusion.1), channel_id=1, source_target_pairs={{0,16},{4,20},{8,24},{12,28},{16,32},{20,36},{24,40},{28,44},{32,4... | collective-permute-start | bytes 196616 | tf_op jit(solution)/shard_map/ppermute | solution.py:14
  102.7 3.9 %gather_fusion = bf16[1024,256]{1,0:T(8,128)(2,1)S(1)} fusion(bf16[128,256]{1,0:T(8,128)(2,1)S(1)} %copy.46, s32[1024]{0:T(1024)S(1)} %get-tuple-element.27), kind=kCustom, calls=%fused_computation.clone | custom fusion | bytes 1052672 | tf_op jit(solution)/shard_map/jit(_take)/gather | solution.py:135
  107.3 3.9 %gather_fusion.1 = bf16[1024,256]{1,0:T(8,128)(2,1)S(1)} fusion(bf16[128,256]{1,0:T(8,128)(2,1)S(1)} %copy.46, s32[1024]{0:T(1024)S(1)} %get-tuple-element.28), kind=kCustom, calls=%fused_computation.1.clone | custom fusion | bytes 1052672 | tf_op jit(solution)/shard_map/jit(_take)/gather | solution.py:135
  111.9 3.2 %pad_maximum_fusion = bf16[2,128,2048]{2,0,1:T(2,128)(2,1)} fusion(bf16[1,128,2048]{2,0,1:T(2,128)(2,1)S(1)} %stack_reshape.9, bf16[1,128,2048]{2,0,1:T(2,128)(2,1)S(1)} %stack_reshape.8), kind=kLoop, calls=%fused_computation.17 | loop fusion | flops 2097152 | bytes 2097152 | tf_op jit(solution)/shard_map/stack | solution.py:138
  115.1 8.1 %all-to-all-start.1 = ((bf16[2,128,2048]{2,0,1:T(2,128)(2,1)}), bf16[2,128,2048]{2,0,1:T(2,128)(2,1)S(1)}, u32[]{:S(2)}, u32[]{:S(2)}) async-start(bf16[2,128,2048]{2,0,1:T(2,128)(2,1)} %pad_maximum_fusion), calls=%async_computation.1 | async-start | bytes 2097152 | tf_op jit(solution)/shard_map/all_to_all | solution.py:138
  123.3 3.1 %collective-permute-start.13 = (bf16[128,256]{0,1:T(8,128)(2,1)S(1)}, bf16[128,256]{0,1:T(8,128)(2,1)S(1)}, u32[]{:S(2)}, u32[]{:S(2)}) collective-permute-start(bf16[128,256]{0,1:T(8,128)(2,1)S(1)} %pad_maximum_fusion.1), channel_id=1, source_target_pairs={{0,12},{4,16},{8,20},{12,24},{16,28},{20,32},{24,36},{28,40},{32,4... | collective-permute-start | bytes 196616 | tf_op jit(solution)/shard_map/ppermute | solution.py:14
  127.2 4.6 %collective-permute-start.14 = (bf16[128,256]{0,1:T(8,128)(2,1)S(1)}, bf16[128,256]{0,1:T(8,128)(2,1)S(1)}, u32[]{:S(2)}, u32[]{:S(2)}) collective-permute-start(bf16[128,256]{0,1:T(8,128)(2,1)S(1)} %pad_maximum_fusion.1), channel_id=1, source_target_pairs={{0,8},{4,12},{8,16},{12,20},{16,24},{20,28},{24,32},{28,36},{32,40... | collective-permute-start | bytes 196616 | tf_op jit(solution)/shard_map/ppermute | solution.py:14
  134.2 13.7 %collective-permute-done.13 = bf16[128,256]{0,1:T(8,128)(2,1)S(1)} collective-permute-done((bf16[128,256]{0,1:T(8,128)(2,1)S(1)}, bf16[128,256]{0,1:T(8,128)(2,1)S(1)}, u32[]{:S(2)}, u32[]{:S(2)}) %collective-permute-start.13) | collective-permute-done | bytes 65568 | tf_op jit(solution)/shard_map/ppermute | solution.py:14
  147.9 2.5 %collective-permute-done.14 = bf16[128,256]{0,1:T(8,128)(2,1)S(1)} collective-permute-done((bf16[128,256]{0,1:T(8,128)(2,1)S(1)}, bf16[128,256]{0,1:T(8,128)(2,1)S(1)}, u32[]{:S(2)}, u32[]{:S(2)}) %collective-permute-start.14) | collective-permute-done | bytes 65568 | tf_op jit(solution)/shard_map/ppermute | solution.py:14
  157.9 49.3 %all-gather.7.cloned.1.call-done = bf16[128,12,384]{2,1,0:T(8,128)(2,1)} async-done(((bf16[1,12,384]{2,1,0:T(8,128)(2,1)}), bf16[128,12,384]{2,1,0:T(8,128)(2,1)}) %all-gather.7.cloned.1.call-update) | async-done | bytes 1179664 | tf_op jit(solution)/shard_map/all_gather | solution.py:112
  214.3 23.6 %reduce-scatter.4.cloned.1.call-done = bf16[384,128]{1,0:T(8,128)(2,1)} async-done(((bf16[1536,128]{1,0:T(8,128)(2,1)}), bf16[384,128]{1,0:T(8,128)(2,1)}) %reduce-scatter.4.cloned.1.call-update) | async-done | bytes 98320
  (118 shorter events, 38.0 us)
Async XLA Ops:
  7.2 143.9 %all-gather.5.cloned.1.call-start = ((), (), s32[]{:S(2)}) async-start(), calls=%async_computation.3 | async-start | bytes 1585152 | tf_op jit(solution)/shard_map/all_gather | solution.py:60
  7.9 51.7 %collective-permute-start = (s32[128]{0:T(128)}, s32[128]{0:T(128)S(1)}, u32[]{:S(2)}, u32[]{:S(2)}) collective-permute-start(s32[128]{0:T(128)} %param.15), channel_id=1, source_target_pairs={{0,32},{4,36},{8,40},{12,44},{16,48},{20,52},{24,56},{28,60},{32,6... | collective-permute-start | bytes 1544 | tf_op jit(solution)/shard_map/ppermute | solution.py:14
  13.8 48.9 %collective-permute-start.1 = (s32[128]{0:T(128)}, s32[128]{0:T(128)S(1)}, u32[]{:S(2)}, u32[]{:S(2)}) collective-permute-start(s32[128]{0:T(128)} %param.15), channel_id=1, source_target_pairs={{0,28},{4,32},{8,36},{12,40},{16,44},{20,48},{24,52},{28,56},{32,6... | collective-permute-start | bytes 1544 | tf_op jit(solution)/shard_map/ppermute | solution.py:14
  17.6 49.7 %collective-permute-start.2 = (s32[128]{0:T(128)}, s32[128]{0:T(128)S(1)}, u32[]{:S(2)}, u32[]{:S(2)}) collective-permute-start(s32[128]{0:T(128)} %param.15), channel_id=1, source_target_pairs={{0,24},{4,28},{8,32},{12,36},{16,40},{20,44},{24,48},{28,52},{32,5... | collective-permute-start | bytes 1544 | tf_op jit(solution)/shard_map/ppermute | solution.py:14
  24.3 45.0 %collective-permute-start.3 = (s32[128]{0:T(128)}, s32[128]{0:T(128)S(1)}, u32[]{:S(2)}, u32[]{:S(2)}) collective-permute-start(s32[128]{0:T(128)} %param.15), channel_id=1, source_target_pairs={{0,20},{4,24},{8,28},{12,32},{16,36},{20,40},{24,44},{28,48},{32,5... | collective-permute-start | bytes 1544 | tf_op jit(solution)/shard_map/ppermute | solution.py:14
  27.5 42.0 %collective-permute-start.4 = (s32[128]{0:T(128)}, s32[128]{0:T(128)S(1)}, u32[]{:S(2)}, u32[]{:S(2)}) collective-permute-start(s32[128]{0:T(128)} %param.15), channel_id=1, source_target_pairs={{0,16},{4,20},{8,24},{12,28},{16,32},{20,36},{24,40},{28,44},{32,4... | collective-permute-start | bytes 1544 | tf_op jit(solution)/shard_map/ppermute | solution.py:14
  33.7 24.0 %copy-start.9 = (s32[128]{0:T(128)S(1)}, s32[128]{0:T(128)}, u32[]{:S(2)}) copy-start(s32[128]{0:T(128)} %param.15) | copy-start | bytes 1540
  33.7 24.1 %copy-start = (bf16[128,1536]{1,0:T(8,128)(2,1)S(1)}, bf16[128,1536]{1,0:T(8,128)(2,1)}, u32[]{:S(2)}) copy-start(bf16[128,1536]{1,0:T(8,128)(2,1)} %param.10) | copy-start | bytes 1179652
  33.7 25.9 %copy-start.6 = (bf16[1536]{0:T(1024)(128)(2,1)S(1)}, bf16[1536]{0:T(1024)(128)(2,1)}, u32[]{:S(2)}) copy-start(bf16[1536]{0:T(1024)(128)(2,1)} %param.11) | copy-start | bytes 9220
  33.7 46.5 %all-to-all-start = ((bf16[128,12,256]{2,1,0:T(8,128)(2,1)}), bf16[128,12,256]{2,1,0:T(8,128)(2,1)S(1)}, u32[]{:S(2)}, u32[]{:S(2)}) async-start(bf16[128,12,256]{2,1,0:T(8,128)(2,1)} %stack.8), calls=%async_computation | async-start | bytes 2097152 | tf_op jit(solution)/shard_map/all_to_all | solution.py:63
  49.4 157.8 %all-gather.7.cloned.1.call-start = ((), (), s32[]{:S(2)}) async-start(), calls=%async_computation.4 | async-start | bytes 1585152 | tf_op jit(solution)/shard_map/all_gather | solution.py:112
  59.6 12.2 %collective-permute-start.5 = (s32[128]{0:T(128)S(1)}, s32[128]{0:T(128)S(1)}, u32[]{:S(2)}, u32[]{:S(2)}) collective-permute-start(s32[128]{0:T(128)S(1)} %copy-done.9), channel_id=1, source_target_pairs={{0,12},{4,16},{8,20},{12,24},{16,28},{20,32},{24,36},{28,40},{32,4... | collective-permute-start | bytes 1544 | tf_op jit(solution)/shard_map/ppermute | solution.py:14
  62.7 9.6 %collective-permute-start.6 = (s32[128]{0:T(128)S(1)}, s32[128]{0:T(128)S(1)}, u32[]{:S(2)}, u32[]{:S(2)}) collective-permute-start(s32[128]{0:T(128)S(1)} %copy-done.9), channel_id=1, source_target_pairs={{0,8},{4,12},{8,16},{12,20},{16,24},{20,28},{24,32},{28,36},{32,40... | collective-permute-start | bytes 1544 | tf_op jit(solution)/shard_map/ppermute | solution.py:14
  67.3 5.0 %collective-permute-start.7 = (s32[128]{0:T(128)S(1)}, s32[128]{0:T(128)S(1)}, u32[]{:S(2)}, u32[]{:S(2)}) collective-permute-start(s32[128]{0:T(128)S(1)} %copy-done.9), channel_id=1, source_target_pairs={{0,4},{4,8},{8,12},{12,16},{16,20},{20,24},{24,28},{28,32},{32,36}... | collective-permute-start | bytes 1544 | tf_op jit(solution)/shard_map/ppermute | solution.py:14
  81.3 42.0 %collective-permute-start.8 = (bf16[128,256]{0,1:T(8,128)(2,1)S(1)}, bf16[128,256]{0,1:T(8,128)(2,1)}, u32[]{:S(2)}, u32[]{:S(2)}) collective-permute-start(bf16[128,256]{0,1:T(8,128)(2,1)S(1)} %pad_maximum_fusion.1), channel_id=1, source_target_pairs={{0,32},{4,36},{8,40},{12,44},{16,48},{20,52},{24,56},{28,60},{32,6... | collective-permute-start | bytes 196616 | tf_op jit(solution)/shard_map/ppermute | solution.py:14
  85.5 41.8 %collective-permute-start.9 = (bf16[128,256]{0,1:T(8,128)(2,1)S(1)}, bf16[128,256]{0,1:T(8,128)(2,1)S(1)}, u32[]{:S(2)}, u32[]{:S(2)}) collective-permute-start(bf16[128,256]{0,1:T(8,128)(2,1)S(1)} %pad_maximum_fusion.1), channel_id=1, source_target_pairs={{0,28},{4,32},{8,36},{12,40},{16,44},{20,48},{24,52},{28,56},{32,6... | collective-permute-start | bytes 196616 | tf_op jit(solution)/shard_map/ppermute | solution.py:14
  89.5 42.3 %collective-permute-start.10 = (bf16[128,256]{0,1:T(8,128)(2,1)S(1)}, bf16[128,256]{0,1:T(8,128)(2,1)S(1)}, u32[]{:S(2)}, u32[]{:S(2)}) collective-permute-start(bf16[128,256]{0,1:T(8,128)(2,1)S(1)} %pad_maximum_fusion.1), channel_id=1, source_target_pairs={{0,24},{4,28},{8,32},{12,36},{16,40},{20,44},{24,48},{28,52},{32,5... | collective-permute-start | bytes 196616 | tf_op jit(solution)/shard_map/ppermute | solution.py:14
  93.2 40.9 %collective-permute-start.11 = (bf16[128,256]{0,1:T(8,128)(2,1)S(1)}, bf16[128,256]{0,1:T(8,128)(2,1)S(1)}, u32[]{:S(2)}, u32[]{:S(2)}) collective-permute-start(bf16[128,256]{0,1:T(8,128)(2,1)S(1)} %pad_maximum_fusion.1), channel_id=1, source_target_pairs={{0,20},{4,24},{8,28},{12,32},{16,36},{20,40},{24,44},{28,48},{32,5... | collective-permute-start | bytes 196616 | tf_op jit(solution)/shard_map/ppermute | solution.py:14
  97.5 36.6 %collective-permute-start.12 = (bf16[128,256]{0,1:T(8,128)(2,1)S(1)}, bf16[128,256]{0,1:T(8,128)(2,1)S(1)}, u32[]{:S(2)}, u32[]{:S(2)}) collective-permute-start(bf16[128,256]{0,1:T(8,128)(2,1)S(1)} %pad_maximum_fusion.1), channel_id=1, source_target_pairs={{0,16},{4,20},{8,24},{12,28},{16,32},{20,36},{24,40},{28,44},{32,4... | collective-permute-start | bytes 196616 | tf_op jit(solution)/shard_map/ppermute | solution.py:14
  115.1 124.5 %all-to-all-start.1 = ((bf16[2,128,2048]{2,0,1:T(2,128)(2,1)}), bf16[2,128,2048]{2,0,1:T(2,128)(2,1)S(1)}, u32[]{:S(2)}, u32[]{:S(2)}) async-start(bf16[2,128,2048]{2,0,1:T(2,128)(2,1)} %pad_maximum_fusion), calls=%async_computation.1 | async-start | bytes 2097152 | tf_op jit(solution)/shard_map/all_to_all | solution.py:138
  123.2 114.7 %reduce-scatter.4.cloned.1.call-start = ((), (), s32[]{:S(2)}) async-start(), calls=%async_computation.5 | async-start | bytes 491520
  123.3 24.6 %collective-permute-start.13 = (bf16[128,256]{0,1:T(8,128)(2,1)S(1)}, bf16[128,256]{0,1:T(8,128)(2,1)S(1)}, u32[]{:S(2)}, u32[]{:S(2)}) collective-permute-start(bf16[128,256]{0,1:T(8,128)(2,1)S(1)} %pad_maximum_fusion.1), channel_id=1, source_target_pairs={{0,12},{4,16},{8,20},{12,24},{16,28},{20,32},{24,36},{28,40},{32,4... | collective-permute-start | bytes 196616 | tf_op jit(solution)/shard_map/ppermute | solution.py:14
  127.2 23.2 %collective-permute-start.14 = (bf16[128,256]{0,1:T(8,128)(2,1)S(1)}, bf16[128,256]{0,1:T(8,128)(2,1)S(1)}, u32[]{:S(2)}, u32[]{:S(2)}) collective-permute-start(bf16[128,256]{0,1:T(8,128)(2,1)S(1)} %pad_maximum_fusion.1), channel_id=1, source_target_pairs={{0,8},{4,12},{8,16},{12,20},{16,24},{20,28},{24,32},{28,36},{32,40... | collective-permute-start | bytes 196616 | tf_op jit(solution)/shard_map/ppermute | solution.py:14
  131.9 19.1 %collective-permute-start.15 = (bf16[128,256]{0,1:T(8,128)(2,1)S(1)}, bf16[128,256]{0,1:T(8,128)(2,1)S(1)}, u32[]{:S(2)}, u32[]{:S(2)}) collective-permute-start(bf16[128,256]{0,1:T(8,128)(2,1)S(1)} %pad_maximum_fusion.1), channel_id=1, source_target_pairs={{0,4},{4,8},{8,12},{12,16},{16,20},{20,24},{24,28},{28,32},{32,36}... | collective-permute-start | bytes 196616 | tf_op jit(solution)/shard_map/ppermute | solution.py:14
  (7 other events, 30.3 us)
Sparse Core Ops, SparseCore 0:
  11.2 104.8 all-gather.4
  119.3 87.8 all-gather.6
  214.3 23.5 reduce-scatter.3
